TPU v7x, 128 devices: a whole 4x4x4 slice. The times are simulated.
128 devices in a mesh: gz: 8 (over z_lo, x), gx: 16 (over y, z_hi, core).
Axes of the slice: x: 4, y: 4, z: 4 (z_hi: 2, z_lo: 2; z = z_hi * 2 + z_lo), core: 2. Of those that a mesh axis runs over, the one named last changes fastest.
Arguments:
- adj_fields: float32 [6, 256, 256, 8, 128], P(None, 'gx', 'gz'), may hold values from -6 to 6
- coef_e: float32 [256, 256, 8, 128], P('gx', 'gz'), may hold values from 0.1 to 0.6
- plane_z: int32 [2], replicated, may hold values from 0 to 255
- snap_index: int32 [1], replicated, may hold values from 0 to 2
- fwd_snaps: float32 [4, 2, 3, 256, 1024], P(None, None, None, 'gx', 'gz'), may hold values from -6 to 6
- design: float32 [2, 256, 1024], P(None, 'gx', 'gz'), may hold values from 0 to 1
- sens_in: float32 [2, 256, 1024], P(None, 'gx', 'gz'), may hold values from -6 to 6
Outputs:
- new_fields: float32 [6, 256, 256, 8, 128], P(None, 'gx', 'gz')
- gradient: float32 [2, 256, 1024], P(None, 'gx', 'gz')
Inputs may be any that keep to these rules, and one draw needn't show every extreme that they name: `plane_z`: the two design planes may lie in the same or in different z slabs.
All inputs are finite; a program needn't handle non-finite values.
Results may differ from a plain program's by a relative error of at most 0.00016.
Values sent between devices are 32-bit elements; how exact they have to be, the bound alone decides.
No kernel may reach another device: no remote copies, remote signals or barrier semaphores. Data moves between devices by JAX's collectives and lax.ppermute only.
A program may use at most 128 MiB of HBM per device.

v0:
```python
import functools
import math

import jax
import jax.numpy as jnp
from jax import lax
from jax.experimental import pallas as pl
from jax.experimental.pallas import tpu as pltpu
from jax.sharding import PartitionSpec as P


R = 8
STEPS = 2
SHARPNESS = 8.0
THRESHOLD = 0.5
HALF = 0.5
F32 = jnp.float32
SUB, LANE = 8, 128
CHUNK = 32
SLOT = 16
COMPS = 6
Z_LINES = 4
X_LINES = 5

VMEM = pl.BlockSpec(memory_space=pltpu.VMEM)
HBM = pl.BlockSpec(memory_space=pltpu.HBM)
SMEM = pl.BlockSpec(memory_space=pltpu.SMEM)


def weight(a, b):
    total = sum(
        max(0.0, R - math.sqrt(i * i + j * j)) for i in range(-R, R + 1) for j in range(-R, R + 1)
    )
    return max(0.0, R - math.sqrt(a * a + b * b)) / total


def call(kernel, outs, ins, out_specs=None, in_specs=None, scratch=(), alias=None, cost=None, limit=8):
    out_specs = out_specs or [VMEM] * len(outs)
    in_specs = in_specs or [VMEM] * len(ins)
    return pl.pallas_call(
        kernel,
        out_shape=outs,
        in_specs=in_specs,
        out_specs=out_specs,
        scratch_shapes=list(scratch),
        input_output_aliases=alias or {},
        cost_estimate=cost,
        compiler_params=pltpu.CompilerParams(vmem_limit_bytes=limit << 20),
    )(*ins)


def vmem(*shape):
    return pltpu.VMEM(shape, F32)


def is_even(axis):
    return lax.rem(lax.axis_index(axis), 2) == 0


def iota(v, dim):
    return lax.broadcasted_iota(jnp.int32, v.shape, dim)


def ahead(v):
    n = v.ndim
    r = pltpu.roll(v, LANE - 1, n - 1)
    s = jnp.where(iota(v, n - 2) == SUB - 1, 0.0, pltpu.roll(r, SUB - 1, n - 2))
    return jnp.where(iota(v, n - 1) == LANE - 1, s, r)


def behind(v):
    n = v.ndim
    r = pltpu.roll(v, 1, n - 1)
    s = jnp.where(iota(v, n - 2) == 0, 0.0, pltpu.roll(r, 1, n - 2))
    return jnp.where(iota(v, n - 1) == 0, s, r)


def part_x(ex, exz, ey, ez, hy, hz):
    return hy + HALF * ((exz - ex) + ez), hz + HALF * (-ey - (ahead(ex) - ex))


def post(first, second, even, rows, forward, backward):
    first[rows] = jnp.where(even, forward, backward)
    second[rows] = jnp.where(even, backward, forward)


def pack_slots(arrays, trailing):
    per = LANE // SLOT
    tiles = []
    for t in range(-(-len(arrays) // per)):
        group = arrays[t * per : (t + 1) * per]
        lane = iota(group[0], 1)
        tile = jnp.zeros_like(group[0])
        for k, v in enumerate(group):
            shift = (SLOT * k + (SLOT if trailing else 0)) % LANE
            moved = pltpu.roll(v, shift, 1) if shift else v
            tile = jnp.where((lane >= SLOT * k) & (lane < SLOT * (k + 1)), moved, tile)
        tiles.append(tile)
    return tiles


def unpack_slot(left_tile, right_tile, k):
    lane = iota(left_tile, 1)
    right = pltpu.roll(right_tile, (LANE - SLOT * k) % LANE, 1) if k else right_tile
    shift = (LANE - SLOT - SLOT * k) % LANE
    left = pltpu.roll(left_tile, shift, 1) if shift else left_tile
    return jnp.where(lane < SLOT, right, jnp.where(lane >= LANE - SLOT, left, 0.0))


def rows_of(v):
    return v.reshape(v.shape[0] // SUB, SUB, LANE)


def flat(v):
    return v.reshape(v.shape[0] * SUB, LANE)


def open_kernel(f, coef, design, sens, snaps, snap_index, za, zb, lo, hi, post_x, ends, sem):
    cells_x, cells_z = f.shape[1], f.shape[2]
    copies = [
        pltpu.make_async_copy(f.at[0:3, :, 0], lo, sem.at[0]),
        pltpu.make_async_copy(f.at[0:5, :, cells_z - 1], hi, sem.at[1]),
        pltpu.make_async_copy(f.at[:, cells_x - 1, 0:2], post_x, sem.at[2]),
        pltpu.make_async_copy(coef.at[0, cells_z - 1], ends.at[0], sem.at[3]),
        pltpu.make_async_copy(coef.at[cells_x - 1, 0], ends.at[1], sem.at[4]),
    ]
    for c in copies:
        c.start()
    even_z = is_even("gz")
    s0 = snap_index[0]
    arrays = [design[0], design[1], sens[0], sens[1]]
    arrays += [snaps[s0 + s, p, c] for s in range(STEPS) for p in range(2) for c in range(3)]
    base = 2 * cells_x + Z_LINES
    tiles = zip(pack_slots(arrays, True), pack_slots(arrays, False))
    for t, (forward, backward) in enumerate(tiles):
        n = forward.shape[0] // SUB
        post(za, zb, even_z, pl.ds(base + n * t, n), rows_of(forward), rows_of(backward))
    for c in copies:
        c.wait()
    z_rows(lo[0], lo[1], hi, za, zb, even_z, cells_x)
    ex, ey, ez, hy, hz = (post_x[c, 0] for c in (0, 1, 2, 4, 5))
    ay, az = part_x(ex, post_x[0, 1], ey, ez, hy, hz)
    zero = jnp.zeros_like(ay)
    upward = (hi[2, 0], ends[0], zero, zero)
    downward = (lo[2, 0], ends[1], ay, az)
    for r in range(Z_LINES):
        post(za, zb, even_z, 2 * cells_x + r, upward[r], downward[r])


def open_x_kernel(f, xa, xb, first, last, sem):
    cells_x, cells_z = f.shape[1], f.shape[2]
    copies = [
        pltpu.make_async_copy(f.at[0:3, 0], first, sem.at[0]),
        pltpu.make_async_copy(f.at[:, cells_x - 1], last, sem.at[1]),
    ]
    for c in copies:
        c.start()
    for c in copies:
        c.wait()
    x_rows(first.at[1:3], 0, last, xa, xb, is_even("gx"), cells_z)
    for o in (xa, xb):
        o[2 * cells_z + X_LINES - 1] = first[0, 0]


def z_rows(ex0, ey0, hi, za, zb, even, cells_x):
    ex, ey, ez, hx, hy = (hi[c] for c in range(5))
    ez_next = jnp.concatenate([ez[1:], jnp.zeros_like(ez[:1])], axis=0)
    bx = hx + HALF * ((ahead(ez) - ez) + ey)
    by = hy + HALF * (-ex - (ez_next - ez))
    post(za, zb, even, pl.ds(0, cells_x), bx, ex0)
    post(za, zb, even, pl.ds(cells_x, cells_x), by, ey0)


def x_rows(first, offset, last, xa, xb, even, cells_z):
    for z in range(0, cells_z, 8):
        n = pl.ds(z, 8)
        ex, ey, ez, hy, hz = (last[c, pl.ds(z + offset, 8)] for c in (0, 1, 2, 4, 5))
        if z + 8 < cells_z:
            exz = last[0, pl.ds(z + offset + 1, 8)]
        else:
            exz = jnp.concatenate([ex[1:], jnp.zeros_like(ex[:1])], axis=0)
        ay, az = part_x(ex, exz, ey, ez, hy, hz)
        post(xa, xb, even, n, ay, first[0, pl.ds(z + offset, 8)])
        post(xa, xb, even, pl.ds(cells_z + z, 8), az, first[1, pl.ds(z + offset, 8)])


def patch_kernel(cells_x, cells_z, za, zb, design, xa, xb, xao, xbo):
    even_z, even_x = is_even("gz"), is_even("gx")
    for r in range(0, 2 * cells_z, 8):
        xao[pl.ds(r, 8)] = xa[pl.ds(r, 8)]
        xbo[pl.ds(r, 8)] = xb[pl.ds(r, 8)]
    above = lambda r: jnp.where(even_z, za[r], zb[r])
    below = lambda r: jnp.where(even_z, zb[r], za[r])
    line = 2 * cells_x
    ex = above(cells_x - 1)
    last = cells_z - 1
    xao[last] = xa[last] + jnp.where(even_x, HALF * ex, 0.0)
    xbo[last] = xb[last] + jnp.where(even_x, 0.0, HALF * ex)
    upward = (above(line + 2), above(line + 3), ex, above(line + 1))
    downward = (below(line), below(0), below(cells_x), below(line + 1))
    at = 2 * cells_z
    for r in range(X_LINES - 1):
        post(xao, xbo, even_x, at + r, upward[r], downward[r])
    xao[at + X_LINES - 1] = xa[at + X_LINES - 1]
    xbo[at + X_LINES - 1] = xb[at + X_LINES - 1]
    rows = at + X_LINES
    base = line + Z_LINES
    n = cells_x // SUB
    tile_a, tile_b = flat(za[pl.ds(base, n)]), flat(zb[pl.ds(base, n)])
    right = jnp.where(even_z, tile_a, tile_b)
    left = jnp.where(even_z, tile_b, tile_a)
    for p in range(2):
        own = rows_of(design[p])
        halo = rows_of(unpack_slot(left, right, p))
        for o, v in ((0, own), (n, halo)):
            xao[pl.ds(rows + 2 * n * p + o, n)] = v
            xbo[pl.ds(rows + 2 * n * p + o, n)] = v


def local_row(plane_z, p, cells_z):
    local = plane_z[p] - lax.axis_index("gz") * cells_z
    return (local >= 0) & (local < cells_z), jnp.clip(local, 0, cells_z - 1)


def update_plane(s, coef, i, electric, cells_z):
    def chunk(k, carry):
        hx_prev, hy_prev = carry
        z = 1 + CHUNK * k
        zs = pl.ds(z, CHUNK)
        ex, ey, ez = s[0, i, zs], s[1, i, zs], s[2, i, zs]
        exz = jnp.concatenate([ex[1:], s[0, i, pl.ds(z + CHUNK, 1)]], axis=0)
        eyz = jnp.concatenate([ey[1:], s[1, i, pl.ds(z + CHUNK, 1)]], axis=0)
        eyx, ezx = s[1, i + 1, zs], s[2, i + 1, zs]
        hx, hy, hz = s[3, i, zs], s[4, i, zs], s[5, i, zs]
        if electric:
            hyx, hzx = s[4, i - 1, zs], s[5, i - 1, zs]
            c = coef[i - 1, pl.ds(CHUNK * k, CHUNK)]
        hx = hx + HALF * ((ahead(ez) - ez) - (eyz - ey))
        hy = hy + HALF * ((exz - ex) - (ezx - ez))
        hz = hz + HALF * ((eyx - ey) - (ahead(ex) - ex))
        s[3, i, zs] = hx
        s[4, i, zs] = hy
        s[5, i, zs] = hz
        if electric:
            put_electric(s, i, zs, c, ex, ey, ez, hx, hy, hz, hx_prev, hy_prev, hyx, hzx)
        return hx[CHUNK - 1 :], hy[CHUNK - 1 :]

    start = (s[3, i, pl.ds(0, 1)], s[4, i, pl.ds(0, 1)])
    lax.fori_loop(0, cells_z // CHUNK, chunk, start)


def put_electric(s, i, zs, c, ex, ey, ez, hx, hy, hz, hx_prev, hy_prev, hyx, hzx):
    hxz = jnp.concatenate([hx_prev, hx[:-1]], axis=0)
    hyz = jnp.concatenate([hy_prev, hy[:-1]], axis=0)
    s[0, i, zs] = ex - c * ((hz - behind(hz)) - (hy - hyz))
    s[1, i, zs] = ey - c * ((hx - hxz) - (hz - hzx))
    s[2, i, zs] = ez - c * ((hy - hyx) - (hx - behind(hx)))


def update_electric(s, coef, i, cells_z):
    def chunk(k, carry):
        hx_prev, hy_prev = carry
        zs = pl.ds(1 + CHUNK * k, CHUNK)
        ex, ey, ez = s[0, i, zs], s[1, i, zs], s[2, i, zs]
        hx, hy, hz = s[3, i, zs], s[4, i, zs], s[5, i, zs]
        hyx, hzx = s[4, i - 1, zs], s[5, i - 1, zs]
        c = coef[i - 1, pl.ds(CHUNK * k, CHUNK)]
        put_electric(s, i, zs, c, ex, ey, ez, hx, hy, hz, hx_prev, hy_prev, hyx, hzx)
        return hx[CHUNK - 1 :], hy[CHUNK - 1 :]

    start = (s[3, i, pl.ds(0, 1)], s[4, i, pl.ds(0, 1)])
    lax.fori_loop(0, cells_z // CHUNK, chunk, start)


def take_z(s, za, zb, i, even, top, cells_x, cells_z):
    j = i - 1
    right_x = jnp.where(even, za[j], zb[j])
    right_y = jnp.where(even, za[cells_x + j], zb[cells_x + j])
    left_x = jnp.where(even, zb[j], za[j])
    left_y = jnp.where(even, zb[cells_x + j], za[cells_x + j])
    s[0, i, cells_z + 1] = right_x
    s[1, i, cells_z + 1] = right_y
    s[3, i, 0] = jnp.where(top, 0.0, left_x - HALF * s[1, i, 1])
    s[4, i, 0] = jnp.where(top, 0.0, left_y + HALF * s[0, i, 1])


def inner_first_kernel(f, coef_in, za, zb, s, coef, sem):
    cells_x, cells_z = f.shape[1], f.shape[2]

    def copies(i):
        return (
            pltpu.make_async_copy(f.at[:, i], s.at[:, i + 1, pl.ds(1, cells_z)], sem.at[0, i]),
            pltpu.make_async_copy(coef_in.at[i], coef.at[i], sem.at[1, i]),
        )

    for i in range(cells_x):
        for c in copies(i):
            c.start()
    even = is_even("gz")
    top = lax.axis_index("gz") == 0

    def wait(i):
        for c in copies(i):
            c.wait()
        take_z(s, za, zb, i + 1, even, top, cells_x, cells_z)

    wait(0)
    wait(1)
    update_plane(s, coef, 1, False, cells_z)

    def plane(i, carry):
        wait(i)
        update_plane(s, coef, i, True, cells_z)
        return carry

    lax.fori_loop(2, cells_x, plane, 0)


def take_x(s, xa, xb, corner, cells_x, cells_z):
    even = is_even("gx")
    edge = lax.axis_index("gx") == 0
    top = lax.axis_index("gz") == 0
    last = cells_x
    for z in range(0, cells_z, 8):
        n, m, pz = pl.ds(z, 8), pl.ds(cells_z + z, 8), pl.ds(z + 1, 8)
        a0, b0, a1, b1 = xa[n], xb[n], xa[m], xb[m]
        s[1, last + 1, pz] = jnp.where(even, a0, b0)
        s[2, last + 1, pz] = jnp.where(even, a1, b1)
        hy = jnp.where(even, b0, a0) - HALF * s[2, 1, pz]
        hz = jnp.where(even, b1, a1) + HALF * s[1, 1, pz]
        s[4, 0, pz] = jnp.where(edge, 0.0, hy)
        s[5, 0, pz] = jnp.where(edge, 0.0, hz)
    s[4, last, 0] = s[4, last, 0] - HALF * jnp.where(top, 0.0, corner)


def corner_lines(s, xa, xb, za, zb, cells_x, cells_z):
    even_x, even_z = is_even("gx"), is_even("gz")
    at = 2 * cells_z
    above = [jnp.where(even_x, xa[at + r], xb[at + r]) for r in range(X_LINES)]
    below = [jnp.where(even_x, xb[at + r], xa[at + r]) for r in range(X_LINES)]
    ez_next = jnp.where(even_z, za[2 * cells_x], zb[2 * cells_x])
    ay, az, ex, c = below[:4]
    hy = ay - HALF * ez_next
    hz = az + HALF * s[1, 1, cells_z + 1]
    s[0, 0, cells_z + 1] = ex - c * ((hz - behind(hz)) - (hy - s[4, 0, cells_z]))
    ez, bx, by, c, ex = above
    hx = bx - HALF * s[1, cells_x + 1, 1]
    hy = by + HALF * ex
    s[2, cells_x + 1, 0] = ez - c * ((hy - s[4, cells_x, 0]) - (hx - behind(hx)))


def outer_planes(s, coef, cells_x, cells_z):
    update_plane(s, coef, cells_x, True, cells_z)
    update_electric(s, coef, 1, cells_z)


def edge_first_kernel(s_in, coef, xa, xb, za, zb, s, za2, zb2, xa2, xb2):
    del s_in
    cells_x, cells_z = coef.shape[0], coef.shape[1]
    even = is_even("gx")
    corner = jnp.where(even, xa[2 * cells_z], xb[2 * cells_z])
    take_x(s, xa, xb, corner, cells_x, cells_z)
    corner_lines(s, xa, xb, za, zb, cells_x, cells_z)
    outer_planes(s, coef, cells_x, cells_z)
    xs = pl.ds(1, cells_x)
    hi = [s[c, xs, cells_z] for c in range(5)]
    z_rows(s[0, xs, 1], s[1, xs, 1], hi, za2, zb2, is_even("gz"), cells_x)
    x_rows(s.at[1:3, 1], 1, s.at[:, cells_x], xa2, xb2, is_even("gx"), cells_z)


def plane_tiles(s, plane_z, tiles):
    cells_x, cells_z = s.shape[1] - 2, s.shape[2] - 2
    for p in range(2):
        own, at = local_row(plane_z, p, cells_z)
        for c in range(3):
            v = jnp.where(own, s[c, pl.ds(1, cells_x), at + 1], 0.0)
            for x in range(cells_x):
                tiles[:, 3 * p + c, x] = v[x]
    lane = lax.broadcasted_iota(jnp.int32, (cells_x, LANE), 1)
    zero = jnp.zeros((cells_x, LANE), F32)
    for g in range(SUB):
        tile = zero
        for k in range(COMPS):
            left = tiles[g - 1, k] if g > 0 else zero
            right = tiles[g + 1, k] if g < SUB - 1 else zero
            halo = jnp.where(lane < R, right, left)
            moved = pltpu.roll(halo, (SLOT * k + R) % LANE, 1)
            tile = jnp.where((lane >= SLOT * k) & (lane < SLOT * (k + 1)), moved, tile)
        tiles[g, COMPS] = tile


def first_tiles_kernel(s_in, plane_z, s, tiles):
    del s_in
    plane_tiles(s, plane_z, tiles)


def inner_second_kernel(s_in, coef, za, zb, s, out, sem):
    del s_in
    cells_x, cells_z = coef.shape[0], coef.shape[1]
    inside = pl.ds(1, cells_z)
    even = is_even("gz")
    top = lax.axis_index("gz") == 0

    def take(i, carry):
        take_z(s, za, zb, i, even, top, cells_x, cells_z)
        return carry

    lax.fori_loop(1, cells_x + 1, take, 0)

    def first():
        return pltpu.make_async_copy(s.at[3:6, 1, inside], out.at[3:6, 0], sem.at[0])

    def copy(i):
        return pltpu.make_async_copy(s.at[:, i, inside], out.at[:, i - 1], sem.at[i - 1])

    update_plane(s, coef, 1, False, cells_z)
    update_plane(s, coef, 2, True, cells_z)
    first().start()

    def plane(i, carry):
        update_plane(s, coef, i, True, cells_z)
        copy(i - 1).start()
        return carry

    lax.fori_loop(3, cells_x, plane, 0)
    copy(cells_x - 1).start()
    first().wait()

    def wait(i, carry):
        copy(i).wait()
        return carry

    lax.fori_loop(2, cells_x, wait, 0)


def edge_second_kernel(s_in, coef, xa, xb, tiles, plane_z, out_in, s, out, *refs):
    del s_in, out_in
    outs, (last, sem) = refs[:SUB], refs[SUB:]
    cells_x, cells_z = coef.shape[0], coef.shape[1]
    take_x(s, xa, xb, s[2, cells_x + 1, 0], cells_x, cells_z)
    diagonal = HALF * s[0, 0, cells_z + 1]
    s[4, 0, cells_z] = s[4, 0, cells_z] + jnp.where(lax.axis_index("gx") == 0, 0.0, diagonal)
    outer_planes(s, coef, cells_x, cells_z)
    inside = pl.ds(1, cells_z)
    copies = [
        pltpu.make_async_copy(s.at[0:3, 1, inside], out.at[0:3, 0], sem.at[0]),
        pltpu.make_async_copy(s.at[:, cells_x, inside], out.at[:, cells_x - 1], sem.at[1]),
    ]
    me = lax.axis_index("gz")
    for k, o in enumerate(outs):
        o[0 : COMPS + 1] = tiles[me ^ k]
    for c in copies:
        c.start()
    plane_tiles(s, plane_z, last)
    for k, o in enumerate(outs):
        o[COMPS + 1 :] = last[me ^ k]
    for c in copies:
        c.wait()


def cone(pad, rows):
    width = LANE
    lane = lax.broadcasted_iota(jnp.int32, (rows, width), 1)
    own, halo = pad
    folded = []
    for v in (own, halo):
        terms = [v[R : R + rows]]
        for a in range(1, R):
            terms.append(v[R + a : R + a + rows] + v[R - a : R - a + rows])
        folded.append(terms)

    def mix(terms, b):
        acc = weight(0, b) * terms[0]
        for a in range(1, R):
            if weight(a, b) > 0.0:
                acc = acc + weight(a, b) * terms[a]
        return acc

    acc_own, acc_halo = mix(folded[0], 0), mix(folded[1], 0)
    for b in range(1, R):
        po, ph = mix(folded[0], b), mix(folded[1], b)
        o_up, h_up = pltpu.roll(po, width - b, 1), pltpu.roll(ph, width - b, 1)
        o_dn, h_dn = pltpu.roll(po, b, 1), pltpu.roll(ph, b, 1)
        keep = lane < width - b
        acc_own = acc_own + jnp.where(keep, o_up, h_up)
        acc_halo = acc_halo + jnp.where(keep, h_up, o_up)
        keep = lane >= b
        acc_own = acc_own + jnp.where(keep, o_dn, h_dn)
        acc_halo = acc_halo + jnp.where(keep, h_dn, o_dn)
    return acc_own, acc_halo


def slope_kernel(cells_x, cells_z, xa, xb, za, zb, design, slope):
    even_x, even_z = is_even("gx"), is_even("gz")
    base, n = 2 * cells_z + X_LINES, cells_x // SUB
    zbase = 2 * cells_x + Z_LINES
    tile_a, tile_b = flat(za[pl.ds(zbase, n)]), flat(zb[pl.ds(zbase, n)])
    right = jnp.where(even_z, tile_a, tile_b)
    left = jnp.where(even_z, tile_b, tile_a)
    scale = math.tanh(SHARPNESS * THRESHOLD) + math.tanh(SHARPNESS * (1.0 - THRESHOLD))
    for p in range(2):
        middle = (design[p], unpack_slot(left, right, p))
        pads = []
        for o in range(2):
            rows = pl.ds(base + 2 * n * p + n * o, n)
            a, b = flat(xa[rows]), flat(xb[rows])
            above = jnp.where(even_x, a, b)
            below = jnp.where(even_x, b, a)
            pads.append(jnp.concatenate([below[cells_x - R :], middle[o], above[:R]], axis=0))
        for o, v in enumerate(cone(pads, cells_x)):
            t = jnp.tanh(SHARPNESS * (v - THRESHOLD))
            slope[p, o] = SHARPNESS * (1.0 - t * t) / scale


def weigh_kernel(cells_x, cells_z, *refs):
    blocks, recv = refs[:SUB], refs[-1]
    za, zb, sens, snaps, slope, snap_index, plane_z, wa, wb, own = refs[SUB:-1]
    for p in range(2):
        sender = lax.div(plane_z[p], cells_z) ^ lax.axis_index("gz")
        for k, block in enumerate(blocks):

            @pl.when(sender == k)
            def _(block=block, p=p):
                recv[p] = block[...]

    even_x, even_z = is_even("gx"), is_even("gz")
    per = LANE // SLOT
    n = cells_x // SUB
    base = 2 * cells_x + Z_LINES
    lefts, rights = [], []
    for t in range(2):
        a, b = flat(za[pl.ds(base + n * t, n)]), flat(zb[pl.ds(base + n * t, n)])
        rights.append(jnp.where(even_z, a, b))
        lefts.append(jnp.where(even_z, b, a))
    s0 = snap_index[0]
    lane = lax.broadcasted_iota(jnp.int32, (cells_x, LANE), 1)
    edge = (lane < R) | (lane >= LANE - R)
    for p in range(2):
        total = sens[p]
        halo = unpack_slot(lefts[0], rights[0], 2 + p)
        for s in range(STEPS):
            acc, acc_halo = jnp.zeros_like(total), jnp.zeros_like(total)
            for c in range(3):
                k = p * 3 + c
                slot = 4 + s * COMPS + k
                acc = acc + snaps[s0 + s, p, c] * recv[p, s * (COMPS + 1) + k]
                tile = recv[p, s * (COMPS + 1) + COMPS]
                shift = (2 * LANE - SLOT * k - R) % LANE
                field = pltpu.roll(tile, shift, 1) if shift else tile
                snap = unpack_slot(lefts[slot // per], rights[slot // per], slot % per)
                acc_halo = acc_halo + snap * field
            total = total + acc
            halo = halo + acc_halo
        w0 = total * slope[p, 0]
        w1 = jnp.where(edge, halo * slope[p, 1], 0.0)
        for o, v in enumerate((w0, w1)):
            own[p, o] = v
            up, down = v[cells_x - R :], v[:R]
            wa[p, o] = jnp.where(even_x, up, down)
            wb[p, o] = jnp.where(even_x, down, up)


def gradient_kernel(own, wa, wb, out):
    even = is_even("gx")
    cells_x = own.shape[2]
    for p in range(2):
        pads = []
        for o in range(2):
            below = jnp.where(even, wb[p, o], wa[p, o])
            above = jnp.where(even, wa[p, o], wb[p, o])
            pads.append(jnp.concatenate([below, own[p, o], above], axis=0))
        out[p] = cone(pads, cells_x)[0]


def swap(inner, outer, axis):
    size = lax.axis_size(axis)
    pairs_in = [(i, i ^ 1) for i in range(size)]
    pairs_out = [(i, i + 1 if i % 2 else i - 1) for i in range(1, size - 1)]
    far = lax.ppermute(outer, axis, pairs_out)
    near = lax.ppermute(inner, axis, pairs_in)
    return near, far


def cost(flops, nbytes):
    return pl.CostEstimate(flops=flops, bytes_accessed=nbytes, transcendentals=0)


def shards(f, coef_in, plane_z, snap_index, snaps, design, sens):
    cx, cz = f.shape[1], f.shape[2]
    zr, xr = 2 * cx, 2 * cz
    extra = 2 * (cx // SUB)
    pieces = cx * SUB * LANE
    state = vmem(6, cx + 2, cz + 2, SUB, LANE)
    dma = pltpu.SemaphoreType.DMA
    field_bytes = f.size * 4

    za, zb = call(
        open_kernel,
        [vmem(zr + Z_LINES + extra, SUB, LANE)] * 2,
        (f, coef_in, design, sens, snaps, snap_index),
        in_specs=[HBM, HBM, VMEM, VMEM, VMEM, SMEM],
        scratch=[
            vmem(3, cx, SUB, LANE),
            vmem(5, cx, SUB, LANE),
            vmem(6, 2, SUB, LANE),
            vmem(2, SUB, LANE),
            dma((5,)),
        ],
        cost=cost(1000000, 2000000),
        limit=56,
    )
    za, zb = swap(za, zb, "gz")
    xa, xb = call(
        open_x_kernel,
        [vmem(xr + X_LINES + 2 * extra, SUB, LANE)] * 2,
        (f,),
        in_specs=[HBM],
        scratch=[vmem(3, cz, SUB, LANE), vmem(6, cz, SUB, LANE), dma((2,))],
        cost=cost(4000000, 4000000),
        limit=56,
    )
    xa, xb = call(
        functools.partial(patch_kernel, cx, cz),
        [vmem(xr + X_LINES + 2 * extra, SUB, LANE)] * 2,
        (za, zb, design, xa, xb),
        alias={3: 0, 4: 1},
        cost=cost(10000, 100000),
    )
    xa, xb = swap(xa, xb, "gx")
    s, coef = call(
        inner_first_kernel,
        [state, vmem(cx, cz, SUB, LANE)],
        (f, coef_in, za, zb),
        in_specs=[HBM, HBM, VMEM, VMEM],
        scratch=[dma((2, cx))],
        cost=cost(60 * pieces * cz, 2 * field_bytes),
        limit=37,
    )
    s, za2, zb2, xa2, xb2 = call(
        edge_first_kernel,
        [state] + [vmem(zr, SUB, LANE)] * 2 + [vmem(xr, SUB, LANE)] * 2,
        (s, coef, xa, xb, za, zb),
        alias={0: 0},
        cost=cost(1000000, 2000000),
    )
    slope = call(
        functools.partial(slope_kernel, cx, cz),
        [vmem(2, 2, cx, LANE)],
        (xa, xb, za, zb, design),
        cost=cost(1000000, 100000),
    )[0]
    za2, zb2 = swap(za2, zb2, "gz")
    s, first_tiles = call(
        first_tiles_kernel,
        [state, vmem(SUB, COMPS + 1, cx, LANE)],
        (s, plane_z),
        in_specs=[VMEM, SMEM],
        alias={0: 0},
        cost=cost(4000000, 4000000),
    )
    xa2, xb2 = swap(xa2, xb2, "gx")
    s, out = call(
        inner_second_kernel,
        [state, jax.ShapeDtypeStruct(f.shape, F32)],
        (s, coef, za2, zb2),
        in_specs=[VMEM] * 4,
        out_specs=[VMEM, HBM],
        scratch=[dma((cx,))],
        alias={0: 0},
        cost=cost(60 * pieces * cz, 2 * field_bytes),
    )
    tiles = STEPS * (COMPS + 1)
    _, out, *send = call(
        edge_second_kernel,
        [state, jax.ShapeDtypeStruct(f.shape, F32)] + [vmem(tiles, cx, LANE)] * SUB,
        (s, coef, xa2, xb2, first_tiles, plane_z, out),
        in_specs=[VMEM] * 5 + [SMEM, HBM],
        out_specs=[VMEM, HBM] + [VMEM] * SUB,
        scratch=[vmem(SUB, COMPS + 1, cx, LANE), dma((2,))],
        alias={0: 0, 6: 1},
        cost=cost(4000000, 4000000),
    )
    recv = list(send)
    for k in (6, 7, 2, 5, 3, 4, 1):
        pairs = [(i, i ^ k) for i in range(SUB)]
        recv[k] = lax.ppermute(send[k], "gz", pairs)
    wa, wb, own = call(
        functools.partial(weigh_kernel, cx, cz),
        [vmem(2, 2, R, LANE)] * 2 + [vmem(2, 2, cx, LANE)],
        (*recv, za, zb, sens, snaps, slope, snap_index, plane_z),
        in_specs=[VMEM] * (SUB + 5) + [SMEM] * 2,
        scratch=[vmem(2, tiles, cx, LANE)],
        cost=cost(100000, 100000),
    )
    wa, wb = swap(wa, wb, "gx")
    gradient = call(
        gradient_kernel,
        [jax.ShapeDtypeStruct((2, cx, LANE), F32)],
        (own, wa, wb),
        cost=cost(1000000, 100000),
    )[0]
    return out, gradient


def solution(mesh):
    in_specs = (
        P(None, "gx", "gz", None, None),
        P("gx", "gz", None, None),
        P(),
        P(),
        P(None, None, None, "gx", "gz"),
        P(None, "gx", "gz"),
        P(None, "gx", "gz"),
    )
    out_specs = (P(None, "gx", "gz", None, None), P(None, "gx", "gz"))
    return jax.shard_map(shards, mesh=mesh, in_specs=in_specs, out_specs=out_specs, check_vma=False)
```

profile of v0, /device:TPU:40, one launch (start us, length us, event | category | flops | bytes accessed | tf_op | source)
XLA Modules:
  0.0 77.8 jit_solution(3580418995470985431)
XLA Ops:
  1.3 2.2 %shard_map.86 = (f32[40,8,128]{2,1,0:T(8,128)S(1)}, f32[40,8,128]{2,1,0:T(8,128)S(1)}) custom-call(f32[6,16,32,8,128]{4,3,2,1,0:T(8,128)} %f.5, f32[16,32,8,128]{3,2,1,0:T(8,128)} %coef_in.1, f32[2,16,128]{2,1,0:T(8,128)} %design.5, f32[2,16,128]{2,1,0:T(8,128)} %refs_10_.1, f32[4,2,3,16,128]{4,3,2,1,0:T(8,128)} %refs_11_.1, s32[1]{0:T(128)S(6)} %copy.23.snap_index.refs_13_), custom_call_target="tpu_custom_call" | custom-call | flops 1000000 | bytes 2000000 | tf_op jit(solution)/shard_map/pallas_call | solution.py:40
  3.5 1.6 %collective-permute-start = (f32[40,8,128]{2,1,0:T(8,128)S(1)}, f32[40,8,128]{2,1,0:T(8,128)S(1)}, u32[]{:S(2)}, u32[]{:S(2)}) collective-permute-start(f32[40,8,128]{2,1,0:T(8,128)S(1)} %get-tuple-element.31), channel_id=1, source_target_pairs={{0,16},{16,0},{32,48},{48,32},{64,80},{80,64},{96,112},{112,96},{1... | collective-permute-start | bytes 491528 | tf_op jit(solution)/shard_map/ppermute | solution.py:580
  5.1 3.5 %collective-permute-start.1 = (f32[40,8,128]{2,1,0:T(8,128)S(1)}, f32[40,8,128]{2,1,0:T(8,128)S(1)}, u32[]{:S(2)}, u32[]{:S(2)}) collective-permute-start(f32[40,8,128]{2,1,0:T(8,128)S(1)} %get-tuple-element.32), channel_id=1, source_target_pairs={{16,32},{32,16},{48,64},{64,48},{80,96},{96,80},{17,33},{33,17},{4... | collective-permute-start | bytes 491528 | tf_op jit(solution)/shard_map/ppermute | solution.py:579
  8.6 1.4 %shard_map.88 = (f32[77,8,128]{2,1,0:T(8,128)S(1)}, f32[77,8,128]{2,1,0:T(8,128)S(1)}) custom-call(f32[6,16,32,8,128]{4,3,2,1,0:T(8,128)} %f.5), custom_call_target="tpu_custom_call" | custom-call | flops 4000000 | bytes 4000000 | tf_op jit(solution)/shard_map/pallas_call | solution.py:40
  10.0 0.0 collective-permute-done.za.refs_8_
  10.0 4.7 %collective-permute-done.1.zb.refs_9_ = f32[40,8,128]{2,1,0:T(8,128)S(1)} collective-permute-done((f32[40,8,128]{2,1,0:T(8,128)S(1)}, f32[40,8,128]{2,1,0:T(8,128)S(1)}, u32[]{:S(2)}, u32[]{:S(2)}) %collective-permute-start.1) | collective-permute-done | bytes 163872 | tf_op jit(solution)/shard_map/ppermute | solution.py:579
  14.7 0.1 shard_map.89
  14.9 0.0 collective-permute-start.2
  14.9 0.0 copy-start.3
  14.9 5.1 %collective-permute-start.3 = (f32[77,8,128]{2,1,0:T(8,128)S(1)}, f32[77,8,128]{2,1,0:T(8,128)S(1)}, u32[]{:S(2)}, u32[]{:S(2)}) collective-permute-start(f32[77,8,128]{2,1,0:T(8,128)S(1)} %get-tuple-element.38), channel_id=1, source_target_pairs={{1,2},{2,1},{3,4},{4,3},{5,6},{6,5},{7,8},{8,7},{9,10},{10,9},{11,... | collective-permute-start | bytes 946184 | tf_op jit(solution)/shard_map/ppermute | solution.py:579
  20.0 6.3 %shard_map.87 = (f32[6,18,34,8,128]{4,3,2,1,0:T(8,128)S(1)}, f32[16,32,8,128]{3,2,1,0:T(8,128)S(1)}) custom-call(f32[6,16,32,8,128]{4,3,2,1,0:T(8,128)} %f.5, f32[16,32,8,128]{3,2,1,0:T(8,128)} %coef_in.1, f32[40,8,128]{2,1,0:T(8,128)S(1)} %collective-permute-done.za.refs_8_, f32[40,8,128]{2,1,0:T(8,128)S(1)} %collective-permute-done.1.zb.refs_9_), custom_call_target="tpu_custom_call" | custom-call | flops 31457280 | bytes 25165824 | tf_op jit(solution)/shard_map/pallas_call | solution.py:40
  26.3 0.0 collective-permute-done.2.xa
  26.3 0.0 collective-permute-done.3.xb
  26.3 0.5 shard_map.90
  26.9 2.5 %collective-permute-start.6 = (f32[64,8,128]{2,1,0:T(8,128)S(1)}, f32[64,8,128]{2,1,0:T(8,128)S(1)}, u32[]{:S(2)}, u32[]{:S(2)}) collective-permute-start(f32[64,8,128]{2,1,0:T(8,128)S(1)} %get-tuple-element.44), channel_id=1, source_target_pairs={{0,1},{1,0},{2,3},{3,2},{4,5},{5,4},{6,7},{7,6},{8,9},{9,8},{10,11... | collective-permute-start | bytes 786440 | tf_op jit(solution)/shard_map/ppermute | solution.py:580
  29.4 4.3 %collective-permute-start.7 = (f32[64,8,128]{2,1,0:T(8,128)S(1)}, f32[64,8,128]{2,1,0:T(8,128)S(1)}, u32[]{:S(2)}, u32[]{:S(2)}) collective-permute-start(f32[64,8,128]{2,1,0:T(8,128)S(1)} %get-tuple-element.45), channel_id=1, source_target_pairs={{1,2},{2,1},{3,4},{4,3},{5,6},{6,5},{7,8},{8,7},{9,10},{10,9},{11,... | collective-permute-start | bytes 786440 | tf_op jit(solution)/shard_map/ppermute | solution.py:579
  33.7 0.1 collective-permute-start.4
  33.8 4.4 %collective-permute-start.5 = (f32[32,8,128]{2,1,0:T(8,128)S(1)}, f32[32,8,128]{2,1,0:T(8,128)S(1)}, u32[]{:S(2)}, u32[]{:S(2)}) collective-permute-start(f32[32,8,128]{2,1,0:T(8,128)S(1)} %get-tuple-element.42), channel_id=1, source_target_pairs={{16,32},{32,16},{48,64},{64,48},{80,96},{96,80},{17,33},{33,17},{4... | collective-permute-start | bytes 393224 | tf_op jit(solution)/shard_map/ppermute | solution.py:579
  38.1 1.0 %shard_map.91 = (f32[6,18,34,8,128]{4,3,2,1,0:T(8,128)S(1)}, f32[8,7,16,128]{3,2,1,0:T(8,128)S(1)}) custom-call(f32[6,18,34,8,128]{4,3,2,1,0:T(8,128)S(1)} %get-tuple-element.39.s_in, s32[2]{0:T(128)S(1)} %copy-done.3), custom_call_target="tpu_custom_call", output_to_operand_aliasing={{0}: (0, {})} | custom-call | flops 4000000 | bytes 4000000 | tf_op jit(solution)/shard_map/pallas_call | solution.py:40
  39.1 0.7 collective-permute-done.4.za
  39.9 4.0 %collective-permute-done.5.zb = f32[32,8,128]{2,1,0:T(8,128)S(1)} collective-permute-done((f32[32,8,128]{2,1,0:T(8,128)S(1)}, f32[32,8,128]{2,1,0:T(8,128)S(1)}, u32[]{:S(2)}, u32[]{:S(2)}) %collective-permute-start.5) | collective-permute-done | bytes 131104 | tf_op jit(solution)/shard_map/ppermute | solution.py:579
  43.9 5.7 %shard_map.92 = (f32[6,18,34,8,128]{4,3,2,1,0:T(8,128)S(1)}, f32[6,16,32,8,128]{4,3,2,1,0:T(8,128)}) custom-call(f32[6,18,34,8,128]{4,3,2,1,0:T(8,128)S(1)} %get-tuple-element.40.s_in, f32[16,32,8,128]{3,2,1,0:T(8,128)S(1)} %get-tuple-element.34.coef, f32[32,8,128]{2,1,0:T(8,128)S(1)} %collective-permute-done.4.za, ...), custom_call_target="tpu_custom_call", output_to_operand_aliasing={{0}: (0, {})} | custom-call | flops 31457280 | bytes 25165824 | tf_op jit(solution)/shard_map/pallas_call | solution.py:40
  49.6 0.0 collective-permute-done.6.xa
  49.6 0.0 collective-permute-done.7.xb
  49.6 0.0 copy-start
  49.6 0.0 copy-start.2
  49.7 2.3 %shard_map.93 = (f32[6,18,34,8,128]{4,3,2,1,0:T(8,128)S(1)}, f32[6,16,32,8,128]{4,3,2,1,0:T(8,128)}, f32[14,16,128]{2,1,0:T(8,128)S(1)}, f32[14,16,128]{2,1,0:T(...) custom-call(f32[6,18,34,8,128]{4,3,2,1,0:T(8,128)S(1)} %get-tuple-el, ...), custom_call_target="tpu_custom_call", output_to_operand_aliasing={{0}: (0, {}), {1}: (6, {})} | custom-call | flops 4000000 | bytes 4000000 | tf_op jit(solution)/shard_map/pallas_call | solution.py:40
  52.0 0.2 collective-permute-start.8
  52.2 0.0 collective-permute-start.9
  52.2 4.6 %collective-permute-start.10 = (f32[14,16,128]{2,1,0:T(8,128)S(1)}, f32[14,16,128]{2,1,0:T(8,128)S(1)}, u32[]{:S(2)}, u32[]{:S(2)}) collective-permute-start(f32[14,16,128]{2,1,0:T(8,128)S(1)} %get-tuple-element.52), channel_id=1, source_target_pairs={{0,48},{16,32},{32,16},{48,0},{64,112},{80,96},{96,80},{112,64},{1... | collective-permute-start | bytes 344072 | tf_op jit(solution)/shard_map/ppermute | solution.py:686
  56.7 0.0 collective-permute-start.11
  56.7 0.4 collective-permute-start.12
  57.1 0.9 %collective-permute-done.8.refs_1_ = f32[14,16,128]{2,1,0:T(8,128)S(1)} collective-permute-done((f32[14,16,128]{2,1,0:T(8,128)S(1)}, f32[14,16,128]{2,1,0:T(8,128)S(1)}, u32[]{:S(2)}, u32[]{:S(2)}) %collective-permute-start.8) | collective-permute-done | bytes 114720 | tf_op jit(solution)/shard_map/ppermute | solution.py:686
  58.1 3.5 %collective-permute-start.13 = (f32[14,16,128]{2,1,0:T(8,128)S(1)}, f32[14,16,128]{2,1,0:T(8,128)S(1)}, u32[]{:S(2)}, u32[]{:S(2)}) collective-permute-start(f32[14,16,128]{2,1,0:T(8,128)S(1)} %get-tuple-element.55), channel_id=1, source_target_pairs={{0,96},{16,112},{32,64},{48,80},{64,32},{80,48},{96,0},{112,16},{1... | collective-permute-start | bytes 344072 | tf_op jit(solution)/shard_map/ppermute | solution.py:686
  61.5 0.0 collective-permute-done.9.refs_2_
  61.5 2.3 %collective-permute-start.14 = (f32[14,16,128]{2,1,0:T(8,128)S(1)}, f32[14,16,128]{2,1,0:T(8,128)S(1)}, u32[]{:S(2)}, u32[]{:S(2)}) collective-permute-start(f32[14,16,128]{2,1,0:T(8,128)S(1)} %get-tuple-element.56), channel_id=1, source_target_pairs={{0,112},{16,96},{32,80},{48,64},{64,48},{80,32},{96,16},{112,0},{1... | collective-permute-start | bytes 344072 | tf_op jit(solution)/shard_map/ppermute | solution.py:686
  63.8 0.3 shard_map.94.refs_12_
  64.2 0.0 collective-permute-done.10.refs_3_
  64.2 3.0 %collective-permute-done.11.refs_4_ = f32[14,16,128]{2,1,0:T(8,128)S(1)} collective-permute-done((f32[14,16,128]{2,1,0:T(8,128)S(1)}, f32[14,16,128]{2,1,0:T(8,128)S(1)}, u32[]{:S(2)}, u32[]{:S(2)}) %collective-permute-start.11) | collective-permute-done | bytes 114720 | tf_op jit(solution)/shard_map/ppermute | solution.py:686
  67.2 0.0 collective-permute-done.12.refs_5_
  67.2 0.0 collective-permute-done.13.refs_6_
  67.2 1.2 %collective-permute-done.14.refs_7_ = f32[14,16,128]{2,1,0:T(8,128)S(1)} collective-permute-done((f32[14,16,128]{2,1,0:T(8,128)S(1)}, f32[14,16,128]{2,1,0:T(8,128)S(1)}, u32[]{:S(2)}, u32[]{:S(2)}) %collective-permute-start.14) | collective-permute-done | bytes 114720 | tf_op jit(solution)/shard_map/ppermute | solution.py:686
  68.5 0.8 %shard_map.95 = (f32[2,2,8,128]{3,2,1,0:T(8,128)S(1)}, f32[2,2,8,128]{3,2,1,0:T(8,128)S(1)}, f32[2,2,16,128]{3,2,1,0:T(8,128)S(1)}) custom-call(f32[14,16,128]{2,1,0:T(8,128)S(1)} %get-tuple-element.49.refs_0_, f32[14,16,128]{2,1,0:T(8,128)S(1)} %collective-permute-done.8.refs_1_, f32[14,16,128]{2,1,0:T(8,128)S(1)} %collective-permute-done.9.refs_2_, ...), custom_call_target="tpu_custom_call" | custom-call | flops 100000 | bytes 100000 | tf_op jit(solution)/shard_map/pallas_call | solution.py:40
  69.3 0.1 collective-permute-start.15
  69.3 1.9 %collective-permute-start.16 = (f32[2,2,8,128]{3,2,1,0:T(8,128)S(1)}, f32[2,2,8,128]{3,2,1,0:T(8,128)S(1)}, u32[]{:S(2)}, u32[]{:S(2)}) collective-permute-start(f32[2,2,8,128]{3,2,1,0:T(8,128)S(1)} %get-tuple-element.59), channel_id=1, source_target_pairs={{1,2},{2,1},{3,4},{4,3},{5,6},{6,5},{7,8},{8,7},{9,10},{10,9},{11,... | collective-permute-start | bytes 49160 | tf_op jit(solution)/shard_map/ppermute | solution.py:579
  71.3 0.0 collective-permute-done.15.wa
  71.3 5.5 %collective-permute-done.16.wb = f32[2,2,8,128]{3,2,1,0:T(8,128)S(1)} collective-permute-done((f32[2,2,8,128]{3,2,1,0:T(8,128)S(1)}, f32[2,2,8,128]{3,2,1,0:T(8,128)S(1)}, u32[]{:S(2)}, u32[]{:S(2)}) %collective-permute-start.16) | collective-permute-done | bytes 16416 | tf_op jit(solution)/shard_map/ppermute | solution.py:579
  76.8 1.0 %shard_map.96 = f32[2,16,128]{2,1,0:T(8,128)} custom-call(f32[2,2,16,128]{3,2,1,0:T(8,128)S(1)} %get-tuple-element.57.own, f32[2,2,8,128]{3,2,1,0:T(8,128)S(1)} %collective-permute-done.15.wa, f32[2,2,8,128]{3,2,1,0:T(8,128)S(1)} %collective-permute-done.16.wb), custom_call_target="tpu_custom_call" | custom-call | flops 1000000 | bytes 100000 | tf_op jit(solution)/shard_map/pallas_call | solution.py:40
  (5 shorter events, 0.0 us)
Async XLA Ops:
  0.6 14.1 %copy-start.1 = (f32[2,16,128]{2,1,0:T(8,128)S(1)}, f32[2,16,128]{2,1,0:T(8,128)}, u32[]{:S(2)}) copy-start(f32[2,16,128]{2,1,0:T(8,128)} %design.5) | copy-start | bytes 49156
  3.5 6.5 %collective-permute-start = (f32[40,8,128]{2,1,0:T(8,128)S(1)}, f32[40,8,128]{2,1,0:T(8,128)S(1)}, u32[]{:S(2)}, u32[]{:S(2)}) collective-permute-start(f32[40,8,128]{2,1,0:T(8,128)S(1)} %get-tuple-element.31), channel_id=1, source_target_pairs={{0,16},{16,0},{32,48},{48,32},{64,80},{80,64},{96,112},{112,96},{1... | collective-permute-start | bytes 491528 | tf_op jit(solution)/shard_map/ppermute | solution.py:580
  5.1 9.7 %collective-permute-start.1 = (f32[40,8,128]{2,1,0:T(8,128)S(1)}, f32[40,8,128]{2,1,0:T(8,128)S(1)}, u32[]{:S(2)}, u32[]{:S(2)}) collective-permute-start(f32[40,8,128]{2,1,0:T(8,128)S(1)} %get-tuple-element.32), channel_id=1, source_target_pairs={{16,32},{32,16},{48,64},{64,48},{80,96},{96,80},{17,33},{33,17},{4... | collective-permute-start | bytes 491528 | tf_op jit(solution)/shard_map/ppermute | solution.py:579
  14.9 11.4 %collective-permute-start.2 = (f32[77,8,128]{2,1,0:T(8,128)S(1)}, f32[77,8,128]{2,1,0:T(8,128)S(1)}, u32[]{:S(2)}, u32[]{:S(2)}) collective-permute-start(f32[77,8,128]{2,1,0:T(8,128)S(1)} %get-tuple-element.37), channel_id=1, source_target_pairs={{0,1},{1,0},{2,3},{3,2},{4,5},{5,4},{6,7},{7,6},{8,9},{9,8},{10,11... | collective-permute-start | bytes 946184 | tf_op jit(solution)/shard_map/ppermute | solution.py:580
  14.9 23.2 %copy-start.3 = (s32[2]{0:T(128)S(1)}, s32[2]{0:T(128)}, u32[]{:S(2)}) copy-start(s32[2]{0:T(128)} %refs_14_.1) | copy-start | bytes 28
  14.9 11.4 %collective-permute-start.3 = (f32[77,8,128]{2,1,0:T(8,128)S(1)}, f32[77,8,128]{2,1,0:T(8,128)S(1)}, u32[]{:S(2)}, u32[]{:S(2)}) collective-permute-start(f32[77,8,128]{2,1,0:T(8,128)S(1)} %get-tuple-element.38), channel_id=1, source_target_pairs={{1,2},{2,1},{3,4},{4,3},{5,6},{6,5},{7,8},{8,7},{9,10},{10,9},{11,... | collective-permute-start | bytes 946184 | tf_op jit(solution)/shard_map/ppermute | solution.py:579
  26.9 22.8 %collective-permute-start.6 = (f32[64,8,128]{2,1,0:T(8,128)S(1)}, f32[64,8,128]{2,1,0:T(8,128)S(1)}, u32[]{:S(2)}, u32[]{:S(2)}) collective-permute-start(f32[64,8,128]{2,1,0:T(8,128)S(1)} %get-tuple-element.44), channel_id=1, source_target_pairs={{0,1},{1,0},{2,3},{3,2},{4,5},{5,4},{6,7},{7,6},{8,9},{9,8},{10,11... | collective-permute-start | bytes 786440 | tf_op jit(solution)/shard_map/ppermute | solution.py:580
  29.4 20.2 %collective-permute-start.7 = (f32[64,8,128]{2,1,0:T(8,128)S(1)}, f32[64,8,128]{2,1,0:T(8,128)S(1)}, u32[]{:S(2)}, u32[]{:S(2)}) collective-permute-start(f32[64,8,128]{2,1,0:T(8,128)S(1)} %get-tuple-element.45), channel_id=1, source_target_pairs={{1,2},{2,1},{3,4},{4,3},{5,6},{6,5},{7,8},{8,7},{9,10},{10,9},{11,... | collective-permute-start | bytes 786440 | tf_op jit(solution)/shard_map/ppermute | solution.py:579
  33.7 6.2 %collective-permute-start.4 = (f32[32,8,128]{2,1,0:T(8,128)S(1)}, f32[32,8,128]{2,1,0:T(8,128)S(1)}, u32[]{:S(2)}, u32[]{:S(2)}) collective-permute-start(f32[32,8,128]{2,1,0:T(8,128)S(1)} %get-tuple-element.41), channel_id=1, source_target_pairs={{0,16},{16,0},{32,48},{48,32},{64,80},{80,64},{96,112},{112,96},{1... | collective-permute-start | bytes 393224 | tf_op jit(solution)/shard_map/ppermute | solution.py:580
  33.8 10.1 %collective-permute-start.5 = (f32[32,8,128]{2,1,0:T(8,128)S(1)}, f32[32,8,128]{2,1,0:T(8,128)S(1)}, u32[]{:S(2)}, u32[]{:S(2)}) collective-permute-start(f32[32,8,128]{2,1,0:T(8,128)S(1)} %get-tuple-element.42), channel_id=1, source_target_pairs={{16,32},{32,16},{48,64},{64,48},{80,96},{96,80},{17,33},{33,17},{4... | collective-permute-start | bytes 393224 | tf_op jit(solution)/shard_map/ppermute | solution.py:579
  49.6 18.8 %copy-start = (f32[4,2,3,16,128]{4,3,2,1,0:T(8,128)S(1)}, f32[4,2,3,16,128]{4,3,2,1,0:T(8,128)}, u32[]{:S(2)}) copy-start(f32[4,2,3,16,128]{4,3,2,1,0:T(8,128)} %refs_11_.1) | copy-start | bytes 589828
  49.6 18.8 %copy-start.2 = (f32[2,16,128]{2,1,0:T(8,128)S(1)}, f32[2,16,128]{2,1,0:T(8,128)}, u32[]{:S(2)}) copy-start(f32[2,16,128]{2,1,0:T(8,128)} %refs_10_.1) | copy-start | bytes 49156
  52.0 6.1 %collective-permute-start.8 = (f32[14,16,128]{2,1,0:T(8,128)S(1)}, f32[14,16,128]{2,1,0:T(8,128)S(1)}, u32[]{:S(2)}, u32[]{:S(2)}) collective-permute-start(f32[14,16,128]{2,1,0:T(8,128)S(1)} %get-tuple-element.50), channel_id=1, source_target_pairs={{0,16},{16,0},{32,48},{48,32},{64,80},{80,64},{96,112},{112,96},{1... | collective-permute-start | bytes 344072 | tf_op jit(solution)/shard_map/ppermute | solution.py:686
  52.2 9.4 %collective-permute-start.9 = (f32[14,16,128]{2,1,0:T(8,128)S(1)}, f32[14,16,128]{2,1,0:T(8,128)S(1)}, u32[]{:S(2)}, u32[]{:S(2)}) collective-permute-start(f32[14,16,128]{2,1,0:T(8,128)S(1)} %get-tuple-element.51), channel_id=1, source_target_pairs={{0,32},{16,48},{32,0},{48,16},{64,96},{80,112},{96,64},{112,80},{1... | collective-permute-start | bytes 344072 | tf_op jit(solution)/shard_map/ppermute | solution.py:686
  52.2 12.0 %collective-permute-start.10 = (f32[14,16,128]{2,1,0:T(8,128)S(1)}, f32[14,16,128]{2,1,0:T(8,128)S(1)}, u32[]{:S(2)}, u32[]{:S(2)}) collective-permute-start(f32[14,16,128]{2,1,0:T(8,128)S(1)} %get-tuple-element.52), channel_id=1, source_target_pairs={{0,48},{16,32},{32,16},{48,0},{64,112},{80,96},{96,80},{112,64},{1... | collective-permute-start | bytes 344072 | tf_op jit(solution)/shard_map/ppermute | solution.py:686
  56.7 10.5 %collective-permute-start.11 = (f32[14,16,128]{2,1,0:T(8,128)S(1)}, f32[14,16,128]{2,1,0:T(8,128)S(1)}, u32[]{:S(2)}, u32[]{:S(2)}) collective-permute-start(f32[14,16,128]{2,1,0:T(8,128)S(1)} %get-tuple-element.53), channel_id=1, source_target_pairs={{0,64},{16,80},{32,96},{48,112},{64,0},{80,16},{96,32},{112,48},{1... | collective-permute-start | bytes 344072 | tf_op jit(solution)/shard_map/ppermute | solution.py:686
  56.7 10.5 %collective-permute-start.12 = (f32[14,16,128]{2,1,0:T(8,128)S(1)}, f32[14,16,128]{2,1,0:T(8,128)S(1)}, u32[]{:S(2)}, u32[]{:S(2)}) collective-permute-start(f32[14,16,128]{2,1,0:T(8,128)S(1)} %get-tuple-element.54), channel_id=1, source_target_pairs={{0,80},{16,64},{32,112},{48,96},{64,16},{80,0},{96,48},{112,32},{1... | collective-permute-start | bytes 344072 | tf_op jit(solution)/shard_map/ppermute | solution.py:686
  58.1 9.2 %collective-permute-start.13 = (f32[14,16,128]{2,1,0:T(8,128)S(1)}, f32[14,16,128]{2,1,0:T(8,128)S(1)}, u32[]{:S(2)}, u32[]{:S(2)}) collective-permute-start(f32[14,16,128]{2,1,0:T(8,128)S(1)} %get-tuple-element.55), channel_id=1, source_target_pairs={{0,96},{16,112},{32,64},{48,80},{64,32},{80,48},{96,0},{112,16},{1... | collective-permute-start | bytes 344072 | tf_op jit(solution)/shard_map/ppermute | solution.py:686
  61.5 6.9 %collective-permute-start.14 = (f32[14,16,128]{2,1,0:T(8,128)S(1)}, f32[14,16,128]{2,1,0:T(8,128)S(1)}, u32[]{:S(2)}, u32[]{:S(2)}) collective-permute-start(f32[14,16,128]{2,1,0:T(8,128)S(1)} %get-tuple-element.56), channel_id=1, source_target_pairs={{0,112},{16,96},{32,80},{48,64},{64,48},{80,32},{96,16},{112,0},{1... | collective-permute-start | bytes 344072 | tf_op jit(solution)/shard_map/ppermute | solution.py:686
  69.3 2.0 %collective-permute-start.15 = (f32[2,2,8,128]{3,2,1,0:T(8,128)S(1)}, f32[2,2,8,128]{3,2,1,0:T(8,128)S(1)}, u32[]{:S(2)}, u32[]{:S(2)}) collective-permute-start(f32[2,2,8,128]{3,2,1,0:T(8,128)S(1)} %get-tuple-element.58), channel_id=1, source_target_pairs={{0,1},{1,0},{2,3},{3,2},{4,5},{5,4},{6,7},{7,6},{8,9},{9,8},{10,11... | collective-permute-start | bytes 49160 | tf_op jit(solution)/shard_map/ppermute | solution.py:580
  69.3 7.5 %collective-permute-start.16 = (f32[2,2,8,128]{3,2,1,0:T(8,128)S(1)}, f32[2,2,8,128]{3,2,1,0:T(8,128)S(1)}, u32[]{:S(2)}, u32[]{:S(2)}) collective-permute-start(f32[2,2,8,128]{3,2,1,0:T(8,128)S(1)} %get-tuple-element.59), channel_id=1, source_target_pairs={{1,2},{2,1},{3,4},{4,3},{5,6},{6,5},{7,8},{8,7},{9,10},{10,9},{11,... | collective-permute-start | bytes 49160 | tf_op jit(solution)/shard_map/ppermute | solution.py:579
where the time goes:
time: 79 us; the launch traced here: 77.8 us
  starting transfers between devices  34.4 us (44%)
  Pallas kernels  21.7 us (27%)
  waiting for transfers between devices  20.2 us (26%)
  between operations  1.51 us (2%)
    pallas_call x11, Pallas kernels, call(): pl.pallas_call(kernel, out_shape=outs, in_specs=in_specs, out_specs=out_s...  21.7 us
    ppermute x5, starting transfers between devices, swap(): far = lax.ppermute(outer, axis, pairs_out)  19.1 us
    ppermute x5, waiting for transfers between devices, swap(): far = lax.ppermute(outer, axis, pairs_out)  14.2 us
    ppermute x7, starting transfers between devices, shards(): recv[k] = lax.ppermute(send[k], 'gz', pairs)  10.9 us
    ppermute x7, waiting for transfers between devices, shards(): recv[k] = lax.ppermute(send[k], 'gz', pairs)  5.21 us
    ppermute x5, starting transfers between devices, swap(): near = lax.ppermute(inner, axis, pairs_in)  4.31 us
  transfers between devices with their start and end apart: 17, of which 7 were waited for; matrix products, arithmetic and copies ran while one was open for 0% of the time, Pallas kernels for 19%

commit v1 on v0

--- a/solution.py
+++ b/solution.py
@@ -115,7 +115,9 @@
     return v.reshape(v.shape[0] * SUB, LANE)
 
 
-def open_kernel(f, coef, design, sens, snaps, snap_index, za, zb, lo, hi, post_x, ends, sem):
+def open_kernel(
+    f, coef, design_in, sens_in, snaps_in, za, zb, design, sens, snaps, lo, hi, post_x, ends, sem
+):
     cells_x, cells_z = f.shape[1], f.shape[2]
     copies = [
         pltpu.make_async_copy(f.at[0:3, :, 0], lo, sem.at[0]),
@@ -123,19 +125,23 @@
         pltpu.make_async_copy(f.at[:, cells_x - 1, 0:2], post_x, sem.at[2]),
         pltpu.make_async_copy(coef.at[0, cells_z - 1], ends.at[0], sem.at[3]),
         pltpu.make_async_copy(coef.at[cells_x - 1, 0], ends.at[1], sem.at[4]),
+        pltpu.make_async_copy(snaps_in, snaps, sem.at[5]),
+        pltpu.make_async_copy(design_in, design, sem.at[6]),
+        pltpu.make_async_copy(sens_in, sens, sem.at[7]),
     ]
     for c in copies:
         c.start()
     even_z = is_even("gz")
-    s0 = snap_index[0]
+    for c in copies[5:]:
+        c.wait()
     arrays = [design[0], design[1], sens[0], sens[1]]
-    arrays += [snaps[s0 + s, p, c] for s in range(STEPS) for p in range(2) for c in range(3)]
+    arrays += [snaps[s, p, c] for s in range(snaps.shape[0]) for p in range(2) for c in range(3)]
     base = 2 * cells_x + Z_LINES
     tiles = zip(pack_slots(arrays, True), pack_slots(arrays, False))
     for t, (forward, backward) in enumerate(tiles):
         n = forward.shape[0] // SUB
         post(za, zb, even_z, pl.ds(base + n * t, n), rows_of(forward), rows_of(backward))
-    for c in copies:
+    for c in copies[:5]:
         c.wait()
     z_rows(lo[0], lo[1], hi, za, zb, even_z, cells_x)
     ex, ey, ez, hy, hz = (post_x[c, 0] for c in (0, 1, 2, 4, 5))
@@ -490,13 +496,26 @@
     return acc_own, acc_halo
 
 
-def slope_kernel(cells_x, cells_z, xa, xb, za, zb, design, slope):
+def slope_kernel(
+    cells_x, cells_z, xa, xb, za, zb, design, snaps, snap_index, slope, pair, pair_halo, halos
+):
     even_x, even_z = is_even("gx"), is_even("gz")
     base, n = 2 * cells_z + X_LINES, cells_x // SUB
     zbase = 2 * cells_x + Z_LINES
     tile_a, tile_b = flat(za[pl.ds(zbase, n)]), flat(zb[pl.ds(zbase, n)])
     right = jnp.where(even_z, tile_a, tile_b)
     left = jnp.where(even_z, tile_b, tile_a)
+    per = LANE // SLOT
+    steps = snaps.shape[0]
+    for t in range(-(-(4 + COMPS * steps) // per)):
+        a, b = flat(za[pl.ds(zbase + n * t, n)]), flat(zb[pl.ds(zbase + n * t, n)])
+        above, below = jnp.where(even_z, a, b), jnp.where(even_z, b, a)
+        for slot in range(max(4, per * t), min(4 + COMPS * steps, per * (t + 1))):
+            s, k = divmod(slot - 4, COMPS)
+            halos[s, k // 3, k % 3] = unpack_slot(below, above, slot % per)
+    for s in range(STEPS):
+        pair[s] = snaps[snap_index[0] + s]
+        pair_halo[s] = halos[snap_index[0] + s]
     scale = math.tanh(SHARPNESS * THRESHOLD) + math.tanh(SHARPNESS * (1.0 - THRESHOLD))
     for p in range(2):
         middle = (design[p], unpack_slot(left, right, p))
@@ -514,7 +533,7 @@
 
 def weigh_kernel(cells_x, cells_z, *refs):
     blocks, recv = refs[:SUB], refs[-1]
-    za, zb, sens, snaps, slope, snap_index, plane_z, wa, wb, own = refs[SUB:-1]
+    za, zb, sens, pair, pair_halo, slope, plane_z, wa, wb, own = refs[SUB:-1]
     for p in range(2):
         sender = lax.div(plane_z[p], cells_z) ^ lax.axis_index("gz")
         for k, block in enumerate(blocks):
@@ -524,31 +543,24 @@
                 recv[p] = block[...]
 
     even_x, even_z = is_even("gx"), is_even("gz")
-    per = LANE // SLOT
     n = cells_x // SUB
-    base = 2 * cells_x + Z_LINES
-    lefts, rights = [], []
-    for t in range(2):
-        a, b = flat(za[pl.ds(base + n * t, n)]), flat(zb[pl.ds(base + n * t, n)])
-        rights.append(jnp.where(even_z, a, b))
-        lefts.append(jnp.where(even_z, b, a))
-    s0 = snap_index[0]
+    first = pl.ds(2 * cells_x + Z_LINES, n)
+    a, b = flat(za[first]), flat(zb[first])
+    right, left = jnp.where(even_z, a, b), jnp.where(even_z, b, a)
     lane = lax.broadcasted_iota(jnp.int32, (cells_x, LANE), 1)
     edge = (lane < R) | (lane >= LANE - R)
     for p in range(2):
         total = sens[p]
-        halo = unpack_slot(lefts[0], rights[0], 2 + p)
+        halo = unpack_slot(left, right, 2 + p)
         for s in range(STEPS):
             acc, acc_halo = jnp.zeros_like(total), jnp.zeros_like(total)
             for c in range(3):
                 k = p * 3 + c
-                slot = 4 + s * COMPS + k
-                acc = acc + snaps[s0 + s, p, c] * recv[p, s * (COMPS + 1) + k]
+                acc = acc + pair[s, p, c] * recv[p, s * (COMPS + 1) + k]
                 tile = recv[p, s * (COMPS + 1) + COMPS]
                 shift = (2 * LANE - SLOT * k - R) % LANE
                 field = pltpu.roll(tile, shift, 1) if shift else tile
-                snap = unpack_slot(lefts[slot // per], rights[slot // per], slot % per)
-                acc_halo = acc_halo + snap * field
+                acc_halo = acc_halo + pair_halo[s, p, c] * field
             total = total + acc
             halo = halo + acc_halo
         w0 = total * slope[p, 0]
@@ -594,17 +606,20 @@
     dma = pltpu.SemaphoreType.DMA
     field_bytes = f.size * 4
 
-    za, zb = call(
+    selected = (STEPS,) + snaps.shape[1:]
+    z_extra = -(-(4 + COMPS * snaps.shape[0]) * SLOT // LANE) * (cx // SUB)
+    za, zb, design, sens, snaps = call(
         open_kernel,
-        [vmem(zr + Z_LINES + extra, SUB, LANE)] * 2,
-        (f, coef_in, design, sens, snaps, snap_index),
-        in_specs=[HBM, HBM, VMEM, VMEM, VMEM, SMEM],
+        [vmem(zr + Z_LINES + z_extra, SUB, LANE)] * 2
+        + [vmem(*design.shape), vmem(*sens.shape), vmem(*snaps.shape)],
+        (f, coef_in, design, sens, snaps),
+        in_specs=[HBM] * 5,
         scratch=[
             vmem(3, cx, SUB, LANE),
             vmem(5, cx, SUB, LANE),
             vmem(6, 2, SUB, LANE),
             vmem(2, SUB, LANE),
-            dma((5,)),
+            dma((8,)),
         ],
         cost=cost(1000000, 2000000),
         limit=56,
@@ -643,12 +658,14 @@
         alias={0: 0},
         cost=cost(1000000, 2000000),
     )
-    slope = call(
+    slope, pair, pair_halo = call(
         functools.partial(slope_kernel, cx, cz),
-        [vmem(2, 2, cx, LANE)],
-        (xa, xb, za, zb, design),
+        [vmem(2, 2, cx, LANE), vmem(*selected), vmem(*selected)],
+        (xa, xb, za, zb, design, snaps, snap_index),
+        in_specs=[VMEM] * 6 + [SMEM],
+        scratch=[vmem(*snaps.shape)],
         cost=cost(1000000, 100000),
-    )[0]
+    )
     za2, zb2 = swap(za2, zb2, "gz")
     s, first_tiles = call(
         first_tiles_kernel,
@@ -687,8 +704,8 @@
     wa, wb, own = call(
         functools.partial(weigh_kernel, cx, cz),
         [vmem(2, 2, R, LANE)] * 2 + [vmem(2, 2, cx, LANE)],
-        (*recv, za, zb, sens, snaps, slope, snap_index, plane_z),
-        in_specs=[VMEM] * (SUB + 5) + [SMEM] * 2,
+        (*recv, za, zb, sens, pair, pair_halo, slope, plane_z),
+        in_specs=[VMEM] * (SUB + 6) + [SMEM],
         scratch=[vmem(2, tiles, cx, LANE)],
         cost=cost(100000, 100000),
     )

time: 79 us -> 77.9 us (0.986)
    ppermute x7, waiting for transfers between devices: 5.21 us -> 4.41 us  [shards(): recv[k] = lax.ppermute(send[k], 'gz', pairs)]
where the time goes in v1:
time: 77.9 us; the launch traced here: 76.7 us
  starting transfers between devices  34.4 us (44%)
  Pallas kernels  21.1 us (27%)
  waiting for transfers between devices  19.8 us (25%)
  between operations  1.49 us (2%)
    pallas_call x11, Pallas kernels, call(): pl.pallas_call(kernel, out_shape=outs, in_specs=in_specs, out_specs=out_s...  21.1 us
    ppermute x5, starting transfers between devices, swap(): far = lax.ppermute(outer, axis, pairs_out)  19.1 us
    ppermute x5, waiting for transfers between devices, swap(): far = lax.ppermute(outer, axis, pairs_out)  14.6 us
    ppermute x7, starting transfers between devices, shards(): recv[k] = lax.ppermute(send[k], 'gz', pairs)  10.9 us
    ppermute x7, waiting for transfers between devices, shards(): recv[k] = lax.ppermute(send[k], 'gz', pairs)  4.41 us
    ppermute x5, starting transfers between devices, swap(): near = lax.ppermute(inner, axis, pairs_in)  4.31 us
  transfers between devices with their start and end apart: 17, of which 7 were waited for; matrix products, arithmetic and copies ran while one was open for 0% of the time, Pallas kernels for 19%

profile of v1, /device:TPU:40, one launch (start us, length us, event | category | flops | bytes accessed | tf_op | source)
XLA Modules:
  0.0 76.7 jit_solution(8288527605369412491)
XLA Ops:
  0.6 1.5 %shard_map.86 = (f32[44,8,128]{2,1,0:T(8,128)S(1)}, f32[44,8,128]{2,1,0:T(8,128)S(1)}, f32[2,16,128]{2,1,0:T(8,128)S(1)}, f32[2,16,128]{2,1,0:T(8,128)S(1)}, f32[4,2,3,16,128]{4,3,2,1,0:T(8,128)S(1)}) custom-call(f32[6,16,32,8,128]{4,3,2,1,0:T(8,128)} %f.5, f32[16,32,8,128]{3,2,1,0:T(8,128)} %coef_in.1, f32[2,16,128]{2,1,0:T(8,128)} %design_in.1, ...), custom_call_target="tpu_custom_call" | custom-call | flops 1000000 | bytes 2000000 | tf_op jit(solution)/shard_map/pallas_call | solution.py:40
  2.2 1.6 %collective-permute-start = (f32[44,8,128]{2,1,0:T(8,128)S(1)}, f32[44,8,128]{2,1,0:T(8,128)S(1)}, u32[]{:S(2)}, u32[]{:S(2)}) collective-permute-start(f32[44,8,128]{2,1,0:T(8,128)S(1)} %get-tuple-element.37), channel_id=1, source_target_pairs={{0,16},{16,0},{32,48},{48,32},{64,80},{80,64},{96,112},{112,96},{1... | collective-permute-start | bytes 540680 | tf_op jit(solution)/shard_map/ppermute | solution.py:592
  3.7 3.5 %collective-permute-start.1 = (f32[44,8,128]{2,1,0:T(8,128)S(1)}, f32[44,8,128]{2,1,0:T(8,128)S(1)}, u32[]{:S(2)}, u32[]{:S(2)}) collective-permute-start(f32[44,8,128]{2,1,0:T(8,128)S(1)} %get-tuple-element.38), channel_id=1, source_target_pairs={{16,32},{32,16},{48,64},{64,48},{80,96},{96,80},{17,33},{33,17},{4... | collective-permute-start | bytes 540680 | tf_op jit(solution)/shard_map/ppermute | solution.py:591
  7.3 1.4 %shard_map.88 = (f32[77,8,128]{2,1,0:T(8,128)S(1)}, f32[77,8,128]{2,1,0:T(8,128)S(1)}) custom-call(f32[6,16,32,8,128]{4,3,2,1,0:T(8,128)} %f.5), custom_call_target="tpu_custom_call" | custom-call | flops 4000000 | bytes 4000000 | tf_op jit(solution)/shard_map/pallas_call | solution.py:40
  8.7 0.0 collective-permute-done.za.refs_8_
  8.7 5.0 %collective-permute-done.1.zb.refs_9_ = f32[44,8,128]{2,1,0:T(8,128)S(1)} collective-permute-done((f32[44,8,128]{2,1,0:T(8,128)S(1)}, f32[44,8,128]{2,1,0:T(8,128)S(1)}, u32[]{:S(2)}, u32[]{:S(2)}) %collective-permute-start.1) | collective-permute-done | bytes 180256 | tf_op jit(solution)/shard_map/ppermute | solution.py:591
  13.7 0.1 shard_map.89
  13.9 0.0 collective-permute-start.2
  13.9 0.0 copy-start
  13.9 5.1 %collective-permute-start.3 = (f32[77,8,128]{2,1,0:T(8,128)S(1)}, f32[77,8,128]{2,1,0:T(8,128)S(1)}, u32[]{:S(2)}, u32[]{:S(2)}) collective-permute-start(f32[77,8,128]{2,1,0:T(8,128)S(1)} %get-tuple-element.45), channel_id=1, source_target_pairs={{1,2},{2,1},{3,4},{4,3},{5,6},{6,5},{7,8},{8,7},{9,10},{10,9},{11,... | collective-permute-start | bytes 946184 | tf_op jit(solution)/shard_map/ppermute | solution.py:591
  19.0 6.3 %shard_map.87 = (f32[6,18,34,8,128]{4,3,2,1,0:T(8,128)S(1)}, f32[16,32,8,128]{3,2,1,0:T(8,128)S(1)}) custom-call(f32[6,16,32,8,128]{4,3,2,1,0:T(8,128)} %f.5, f32[16,32,8,128]{3,2,1,0:T(8,128)} %coef_in.1, f32[44,8,128]{2,1,0:T(8,128)S(1)} %collective-permute-done.za.refs_8_, f32[44,8,128]{2,1,0:T(8,128)S(1)} %collective-permute-done.1.zb.refs_9_), custom_call_target="tpu_custom_call" | custom-call | flops 31457280 | bytes 25165824 | tf_op jit(solution)/shard_map/pallas_call | solution.py:40
  25.3 0.0 collective-permute-done.2.xa
  25.3 0.0 collective-permute-done.3.xb
  25.3 0.5 shard_map.90
  25.9 2.5 %collective-permute-start.6 = (f32[64,8,128]{2,1,0:T(8,128)S(1)}, f32[64,8,128]{2,1,0:T(8,128)S(1)}, u32[]{:S(2)}, u32[]{:S(2)}) collective-permute-start(f32[64,8,128]{2,1,0:T(8,128)S(1)} %get-tuple-element.51), channel_id=1, source_target_pairs={{0,1},{1,0},{2,3},{3,2},{4,5},{5,4},{6,7},{7,6},{8,9},{9,8},{10,11... | collective-permute-start | bytes 786440 | tf_op jit(solution)/shard_map/ppermute | solution.py:592
  28.4 4.3 %collective-permute-start.7 = (f32[64,8,128]{2,1,0:T(8,128)S(1)}, f32[64,8,128]{2,1,0:T(8,128)S(1)}, u32[]{:S(2)}, u32[]{:S(2)}) collective-permute-start(f32[64,8,128]{2,1,0:T(8,128)S(1)} %get-tuple-element.52), channel_id=1, source_target_pairs={{1,2},{2,1},{3,4},{4,3},{5,6},{6,5},{7,8},{8,7},{9,10},{10,9},{11,... | collective-permute-start | bytes 786440 | tf_op jit(solution)/shard_map/ppermute | solution.py:591
  32.7 0.1 collective-permute-start.4
  32.8 4.4 %collective-permute-start.5 = (f32[32,8,128]{2,1,0:T(8,128)S(1)}, f32[32,8,128]{2,1,0:T(8,128)S(1)}, u32[]{:S(2)}, u32[]{:S(2)}) collective-permute-start(f32[32,8,128]{2,1,0:T(8,128)S(1)} %get-tuple-element.49), channel_id=1, source_target_pairs={{16,32},{32,16},{48,64},{64,48},{80,96},{96,80},{17,33},{33,17},{4... | collective-permute-start | bytes 393224 | tf_op jit(solution)/shard_map/ppermute | solution.py:591
  37.1 0.0 copy-done
  37.1 1.0 %shard_map.91 = (f32[6,18,34,8,128]{4,3,2,1,0:T(8,128)S(1)}, f32[8,7,16,128]{3,2,1,0:T(8,128)S(1)}) custom-call(f32[6,18,34,8,128]{4,3,2,1,0:T(8,128)S(1)} %get-tuple-element.46.s_in, s32[2]{0:T(128)S(1)} %copy-done), custom_call_target="tpu_custom_call", output_to_operand_aliasing={{0}: (0, {})} | custom-call | flops 4000000 | bytes 4000000 | tf_op jit(solution)/shard_map/pallas_call | solution.py:40
  38.1 0.7 collective-permute-done.4.za
  38.9 4.0 %collective-permute-done.5.zb = f32[32,8,128]{2,1,0:T(8,128)S(1)} collective-permute-done((f32[32,8,128]{2,1,0:T(8,128)S(1)}, f32[32,8,128]{2,1,0:T(8,128)S(1)}, u32[]{:S(2)}, u32[]{:S(2)}) %collective-permute-start.5) | collective-permute-done | bytes 131104 | tf_op jit(solution)/shard_map/ppermute | solution.py:591
  42.9 5.7 %shard_map.92 = (f32[6,18,34,8,128]{4,3,2,1,0:T(8,128)S(1)}, f32[6,16,32,8,128]{4,3,2,1,0:T(8,128)}) custom-call(f32[6,18,34,8,128]{4,3,2,1,0:T(8,128)S(1)} %get-tuple-element.47.s_in, f32[16,32,8,128]{3,2,1,0:T(8,128)S(1)} %get-tuple-element.40.coef, f32[32,8,128]{2,1,0:T(8,128)S(1)} %collective-permute-done.4.za, ...), custom_call_target="tpu_custom_call", output_to_operand_aliasing={{0}: (0, {})} | custom-call | flops 31457280 | bytes 25165824 | tf_op jit(solution)/shard_map/pallas_call | solution.py:40
  48.6 0.0 collective-permute-done.6.xa
  48.6 0.0 collective-permute-done.7.xb
  48.7 2.3 %shard_map.93 = (f32[6,18,34,8,128]{4,3,2,1,0:T(8,128)S(1)}, f32[6,16,32,8,128]{4,3,2,1,0:T(8,128)}, f32[14,16,128]{2,1,0:T(8,128)S(1)}, f32[14,16,128]{2,1,0:T(...) custom-call(f32[6,18,34,8,128]{4,3,2,1,0:T(8,128)S(1)} %get-tuple-el, ...), custom_call_target="tpu_custom_call", output_to_operand_aliasing={{0}: (0, {}), {1}: (6, {})} | custom-call | flops 4000000 | bytes 4000000 | tf_op jit(solution)/shard_map/pallas_call | solution.py:40
  51.0 0.2 collective-permute-start.8
  51.2 0.0 collective-permute-start.9
  51.2 4.6 %collective-permute-start.10 = (f32[14,16,128]{2,1,0:T(8,128)S(1)}, f32[14,16,128]{2,1,0:T(8,128)S(1)}, u32[]{:S(2)}, u32[]{:S(2)}) collective-permute-start(f32[14,16,128]{2,1,0:T(8,128)S(1)} %get-tuple-element.59), channel_id=1, source_target_pairs={{0,48},{16,32},{32,16},{48,0},{64,112},{80,96},{96,80},{112,64},{1... | collective-permute-start | bytes 344072 | tf_op jit(solution)/shard_map/ppermute | solution.py:703
  55.7 0.0 collective-permute-start.11
  55.7 0.4 collective-permute-start.12
  56.1 0.9 %collective-permute-done.8.refs_1_ = f32[14,16,128]{2,1,0:T(8,128)S(1)} collective-permute-done((f32[14,16,128]{2,1,0:T(8,128)S(1)}, f32[14,16,128]{2,1,0:T(8,128)S(1)}, u32[]{:S(2)}, u32[]{:S(2)}) %collective-permute-start.8) | collective-permute-done | bytes 114720 | tf_op jit(solution)/shard_map/ppermute | solution.py:703
  57.1 3.5 %collective-permute-start.13 = (f32[14,16,128]{2,1,0:T(8,128)S(1)}, f32[14,16,128]{2,1,0:T(8,128)S(1)}, u32[]{:S(2)}, u32[]{:S(2)}) collective-permute-start(f32[14,16,128]{2,1,0:T(8,128)S(1)} %get-tuple-element.62), channel_id=1, source_target_pairs={{0,96},{16,112},{32,64},{48,80},{64,32},{80,48},{96,0},{112,16},{1... | collective-permute-start | bytes 344072 | tf_op jit(solution)/shard_map/ppermute | solution.py:703
  60.5 0.0 collective-permute-done.9.refs_2_
  60.5 2.3 %collective-permute-start.14 = (f32[14,16,128]{2,1,0:T(8,128)S(1)}, f32[14,16,128]{2,1,0:T(8,128)S(1)}, u32[]{:S(2)}, u32[]{:S(2)}) collective-permute-start(f32[14,16,128]{2,1,0:T(8,128)S(1)} %get-tuple-element.63), channel_id=1, source_target_pairs={{0,112},{16,96},{32,80},{48,64},{64,48},{80,32},{96,16},{112,0},{1... | collective-permute-start | bytes 344072 | tf_op jit(solution)/shard_map/ppermute | solution.py:703
  63.5 0.5 shard_map.94
  64.0 0.0 collective-permute-done.10.refs_3_
  64.0 2.2 %collective-permute-done.11.refs_4_ = f32[14,16,128]{2,1,0:T(8,128)S(1)} collective-permute-done((f32[14,16,128]{2,1,0:T(8,128)S(1)}, f32[14,16,128]{2,1,0:T(8,128)S(1)}, u32[]{:S(2)}, u32[]{:S(2)}) %collective-permute-start.11) | collective-permute-done | bytes 114720 | tf_op jit(solution)/shard_map/ppermute | solution.py:703
  66.2 0.0 collective-permute-done.12.refs_5_
  66.2 0.0 collective-permute-done.13.refs_6_
  66.2 1.2 %collective-permute-done.14.refs_7_ = f32[14,16,128]{2,1,0:T(8,128)S(1)} collective-permute-done((f32[14,16,128]{2,1,0:T(8,128)S(1)}, f32[14,16,128]{2,1,0:T(8,128)S(1)}, u32[]{:S(2)}, u32[]{:S(2)}) %collective-permute-start.14) | collective-permute-done | bytes 114720 | tf_op jit(solution)/shard_map/ppermute | solution.py:703
  67.5 0.7 shard_map.95
  68.2 0.1 collective-permute-start.15
  68.3 1.9 %collective-permute-start.16 = (f32[2,2,8,128]{3,2,1,0:T(8,128)S(1)}, f32[2,2,8,128]{3,2,1,0:T(8,128)S(1)}, u32[]{:S(2)}, u32[]{:S(2)}) collective-permute-start(f32[2,2,8,128]{3,2,1,0:T(8,128)S(1)} %get-tuple-element.71), channel_id=1, source_target_pairs={{1,2},{2,1},{3,4},{4,3},{5,6},{6,5},{7,8},{8,7},{9,10},{10,9},{11,... | collective-permute-start | bytes 49160 | tf_op jit(solution)/shard_map/ppermute | solution.py:591
  70.2 0.0 collective-permute-done.15.wa
  70.2 5.5 %collective-permute-done.16.wb = f32[2,2,8,128]{3,2,1,0:T(8,128)S(1)} collective-permute-done((f32[2,2,8,128]{3,2,1,0:T(8,128)S(1)}, f32[2,2,8,128]{3,2,1,0:T(8,128)S(1)}, u32[]{:S(2)}, u32[]{:S(2)}) %collective-permute-start.16) | collective-permute-done | bytes 16416 | tf_op jit(solution)/shard_map/ppermute | solution.py:591
  75.8 1.0 %shard_map.96 = f32[2,16,128]{2,1,0:T(8,128)} custom-call(f32[2,2,16,128]{3,2,1,0:T(8,128)S(1)} %get-tuple-element.69.own, f32[2,2,8,128]{3,2,1,0:T(8,128)S(1)} %collective-permute-done.15.wa, f32[2,2,8,128]{3,2,1,0:T(8,128)S(1)} %collective-permute-done.16.wb), custom_call_target="tpu_custom_call" | custom-call | flops 1000000 | bytes 100000 | tf_op jit(solution)/shard_map/pallas_call | solution.py:40
Async XLA Ops:
  2.2 6.5 %collective-permute-start = (f32[44,8,128]{2,1,0:T(8,128)S(1)}, f32[44,8,128]{2,1,0:T(8,128)S(1)}, u32[]{:S(2)}, u32[]{:S(2)}) collective-permute-start(f32[44,8,128]{2,1,0:T(8,128)S(1)} %get-tuple-element.37), channel_id=1, source_target_pairs={{0,16},{16,0},{32,48},{48,32},{64,80},{80,64},{96,112},{112,96},{1... | collective-permute-start | bytes 540680 | tf_op jit(solution)/shard_map/ppermute | solution.py:592
  3.7 10.0 %collective-permute-start.1 = (f32[44,8,128]{2,1,0:T(8,128)S(1)}, f32[44,8,128]{2,1,0:T(8,128)S(1)}, u32[]{:S(2)}, u32[]{:S(2)}) collective-permute-start(f32[44,8,128]{2,1,0:T(8,128)S(1)} %get-tuple-element.38), channel_id=1, source_target_pairs={{16,32},{32,16},{48,64},{64,48},{80,96},{96,80},{17,33},{33,17},{4... | collective-permute-start | bytes 540680 | tf_op jit(solution)/shard_map/ppermute | solution.py:591
  13.9 11.4 %collective-permute-start.2 = (f32[77,8,128]{2,1,0:T(8,128)S(1)}, f32[77,8,128]{2,1,0:T(8,128)S(1)}, u32[]{:S(2)}, u32[]{:S(2)}) collective-permute-start(f32[77,8,128]{2,1,0:T(8,128)S(1)} %get-tuple-element.44), channel_id=1, source_target_pairs={{0,1},{1,0},{2,3},{3,2},{4,5},{5,4},{6,7},{7,6},{8,9},{9,8},{10,11... | collective-permute-start | bytes 946184 | tf_op jit(solution)/shard_map/ppermute | solution.py:592
  13.9 23.2 %copy-start = (s32[2]{0:T(128)S(1)}, s32[2]{0:T(128)}, u32[]{:S(2)}) copy-start(s32[2]{0:T(128)} %refs_14_.1) | copy-start | bytes 28
  13.9 11.4 %collective-permute-start.3 = (f32[77,8,128]{2,1,0:T(8,128)S(1)}, f32[77,8,128]{2,1,0:T(8,128)S(1)}, u32[]{:S(2)}, u32[]{:S(2)}) collective-permute-start(f32[77,8,128]{2,1,0:T(8,128)S(1)} %get-tuple-element.45), channel_id=1, source_target_pairs={{1,2},{2,1},{3,4},{4,3},{5,6},{6,5},{7,8},{8,7},{9,10},{10,9},{11,... | collective-permute-start | bytes 946184 | tf_op jit(solution)/shard_map/ppermute | solution.py:591
  25.9 22.8 %collective-permute-start.6 = (f32[64,8,128]{2,1,0:T(8,128)S(1)}, f32[64,8,128]{2,1,0:T(8,128)S(1)}, u32[]{:S(2)}, u32[]{:S(2)}) collective-permute-start(f32[64,8,128]{2,1,0:T(8,128)S(1)} %get-tuple-element.51), channel_id=1, source_target_pairs={{0,1},{1,0},{2,3},{3,2},{4,5},{5,4},{6,7},{7,6},{8,9},{9,8},{10,11... | collective-permute-start | bytes 786440 | tf_op jit(solution)/shard_map/ppermute | solution.py:592
  28.4 20.2 %collective-permute-start.7 = (f32[64,8,128]{2,1,0:T(8,128)S(1)}, f32[64,8,128]{2,1,0:T(8,128)S(1)}, u32[]{:S(2)}, u32[]{:S(2)}) collective-permute-start(f32[64,8,128]{2,1,0:T(8,128)S(1)} %get-tuple-element.52), channel_id=1, source_target_pairs={{1,2},{2,1},{3,4},{4,3},{5,6},{6,5},{7,8},{8,7},{9,10},{10,9},{11,... | collective-permute-start | bytes 786440 | tf_op jit(solution)/shard_map/ppermute | solution.py:591
  32.7 6.2 %collective-permute-start.4 = (f32[32,8,128]{2,1,0:T(8,128)S(1)}, f32[32,8,128]{2,1,0:T(8,128)S(1)}, u32[]{:S(2)}, u32[]{:S(2)}) collective-permute-start(f32[32,8,128]{2,1,0:T(8,128)S(1)} %get-tuple-element.48), channel_id=1, source_target_pairs={{0,16},{16,0},{32,48},{48,32},{64,80},{80,64},{96,112},{112,96},{1... | collective-permute-start | bytes 393224 | tf_op jit(solution)/shard_map/ppermute | solution.py:592
  32.8 10.1 %collective-permute-start.5 = (f32[32,8,128]{2,1,0:T(8,128)S(1)}, f32[32,8,128]{2,1,0:T(8,128)S(1)}, u32[]{:S(2)}, u32[]{:S(2)}) collective-permute-start(f32[32,8,128]{2,1,0:T(8,128)S(1)} %get-tuple-element.49), channel_id=1, source_target_pairs={{16,32},{32,16},{48,64},{64,48},{80,96},{96,80},{17,33},{33,17},{4... | collective-permute-start | bytes 393224 | tf_op jit(solution)/shard_map/ppermute | solution.py:591
  51.0 6.1 %collective-permute-start.8 = (f32[14,16,128]{2,1,0:T(8,128)S(1)}, f32[14,16,128]{2,1,0:T(8,128)S(1)}, u32[]{:S(2)}, u32[]{:S(2)}) collective-permute-start(f32[14,16,128]{2,1,0:T(8,128)S(1)} %get-tuple-element.57), channel_id=1, source_target_pairs={{0,16},{16,0},{32,48},{48,32},{64,80},{80,64},{96,112},{112,96},{1... | collective-permute-start | bytes 344072 | tf_op jit(solution)/shard_map/ppermute | solution.py:703
  51.2 9.4 %collective-permute-start.9 = (f32[14,16,128]{2,1,0:T(8,128)S(1)}, f32[14,16,128]{2,1,0:T(8,128)S(1)}, u32[]{:S(2)}, u32[]{:S(2)}) collective-permute-start(f32[14,16,128]{2,1,0:T(8,128)S(1)} %get-tuple-element.58), channel_id=1, source_target_pairs={{0,32},{16,48},{32,0},{48,16},{64,96},{80,112},{96,64},{112,80},{1... | collective-permute-start | bytes 344072 | tf_op jit(solution)/shard_map/ppermute | solution.py:703
  51.2 12.8 %collective-permute-start.10 = (f32[14,16,128]{2,1,0:T(8,128)S(1)}, f32[14,16,128]{2,1,0:T(8,128)S(1)}, u32[]{:S(2)}, u32[]{:S(2)}) collective-permute-start(f32[14,16,128]{2,1,0:T(8,128)S(1)} %get-tuple-element.59), channel_id=1, source_target_pairs={{0,48},{16,32},{32,16},{48,0},{64,112},{80,96},{96,80},{112,64},{1... | collective-permute-start | bytes 344072 | tf_op jit(solution)/shard_map/ppermute | solution.py:703
  55.7 10.5 %collective-permute-start.11 = (f32[14,16,128]{2,1,0:T(8,128)S(1)}, f32[14,16,128]{2,1,0:T(8,128)S(1)}, u32[]{:S(2)}, u32[]{:S(2)}) collective-permute-start(f32[14,16,128]{2,1,0:T(8,128)S(1)} %get-tuple-element.60), channel_id=1, source_target_pairs={{0,64},{16,80},{32,96},{48,112},{64,0},{80,16},{96,32},{112,48},{1... | collective-permute-start | bytes 344072 | tf_op jit(solution)/shard_map/ppermute | solution.py:703
  55.7 10.5 %collective-permute-start.12 = (f32[14,16,128]{2,1,0:T(8,128)S(1)}, f32[14,16,128]{2,1,0:T(8,128)S(1)}, u32[]{:S(2)}, u32[]{:S(2)}) collective-permute-start(f32[14,16,128]{2,1,0:T(8,128)S(1)} %get-tuple-element.61), channel_id=1, source_target_pairs={{0,80},{16,64},{32,112},{48,96},{64,16},{80,0},{96,48},{112,32},{1... | collective-permute-start | bytes 344072 | tf_op jit(solution)/shard_map/ppermute | solution.py:703
  57.1 9.2 %collective-permute-start.13 = (f32[14,16,128]{2,1,0:T(8,128)S(1)}, f32[14,16,128]{2,1,0:T(8,128)S(1)}, u32[]{:S(2)}, u32[]{:S(2)}) collective-permute-start(f32[14,16,128]{2,1,0:T(8,128)S(1)} %get-tuple-element.62), channel_id=1, source_target_pairs={{0,96},{16,112},{32,64},{48,80},{64,32},{80,48},{96,0},{112,16},{1... | collective-permute-start | bytes 344072 | tf_op jit(solution)/shard_map/ppermute | solution.py:703
  60.5 6.9 %collective-permute-start.14 = (f32[14,16,128]{2,1,0:T(8,128)S(1)}, f32[14,16,128]{2,1,0:T(8,128)S(1)}, u32[]{:S(2)}, u32[]{:S(2)}) collective-permute-start(f32[14,16,128]{2,1,0:T(8,128)S(1)} %get-tuple-element.63), channel_id=1, source_target_pairs={{0,112},{16,96},{32,80},{48,64},{64,48},{80,32},{96,16},{112,0},{1... | collective-permute-start | bytes 344072 | tf_op jit(solution)/shard_map/ppermute | solution.py:703
  68.2 2.0 %collective-permute-start.15 = (f32[2,2,8,128]{3,2,1,0:T(8,128)S(1)}, f32[2,2,8,128]{3,2,1,0:T(8,128)S(1)}, u32[]{:S(2)}, u32[]{:S(2)}) collective-permute-start(f32[2,2,8,128]{3,2,1,0:T(8,128)S(1)} %get-tuple-element.70), channel_id=1, source_target_pairs={{0,1},{1,0},{2,3},{3,2},{4,5},{5,4},{6,7},{7,6},{8,9},{9,8},{10,11... | collective-permute-start | bytes 49160 | tf_op jit(solution)/shard_map/ppermute | solution.py:592
  68.3 7.5 %collective-permute-start.16 = (f32[2,2,8,128]{3,2,1,0:T(8,128)S(1)}, f32[2,2,8,128]{3,2,1,0:T(8,128)S(1)}, u32[]{:S(2)}, u32[]{:S(2)}) collective-permute-start(f32[2,2,8,128]{3,2,1,0:T(8,128)S(1)} %get-tuple-element.71), channel_id=1, source_target_pairs={{1,2},{2,1},{3,4},{4,3},{5,6},{6,5},{7,8},{8,7},{9,10},{10,9},{11,... | collective-permute-start | bytes 49160 | tf_op jit(solution)/shard_map/ppermute | solution.py:591
